TPU v7x, 256 devices: a whole 4x4x8 slice. The times are simulated.
256 devices in a mesh: dp: 32 (over z_hi, x, core), tensor: 8 (over z_lo, y).
Axes of the slice: x: 4, y: 4, z: 8 (z_hi: 4, z_lo: 2; z = z_hi * 2 + z_lo), core: 2. Of those that a mesh axis runs over, the one named last changes fastest.
Arguments:
- quant_rows: int32 [32768, 2048], P(('dp', 'tensor')), may hold values from -127 to 127
- residual: bfloat16 [32768, 2048], P(('dp', 'tensor')), may hold values from -48 to 48
- row_scale: float32 [32768], P(('dp', 'tensor')), may hold values from 0.004 to 0.04
- norm_gain: float32 [2048], replicated, may hold values from 0.1 to 1.9
- gate_pre: bfloat16 [32768, 7168], P('dp', 'tensor'), may hold values from -6 to 6
- up_pre: bfloat16 [32768, 7168], P('dp', 'tensor'), may hold values from -6 to 6
- hidden_grad: bfloat16 [32768, 7168], P('dp', 'tensor'), may hold values from -6 to 6
- gate_weight: bfloat16 [2048, 7168], P('dp', 'tensor'), may hold values from -0.125 to 0.125
- up_weight: bfloat16 [2048, 7168], P('dp', 'tensor'), may hold values from -0.125 to 0.125
Outputs:
- resid_grad: bfloat16 [32768, 2048], P(('dp', 'tensor'))
- gate_weight_grad: float32 [2048, 7168], P('dp', 'tensor')
- up_weight_grad: float32 [2048, 7168], P('dp', 'tensor')
All inputs are finite; a program needn't handle non-finite values.
Results may differ from a plain program's by a relative error of at most 0.014.
Values may be sent and summed in bfloat16 or wider, within the bound.
No kernel may reach another device: no remote copies, remote signals or barrier semaphores. Data moves between devices by JAX's collectives and lax.ppermute only.
A program may use at most 64 MiB of HBM per device.

v0:
```python
import math

import jax
import jax.numpy as jnp
from jax import lax
from jax.experimental import pallas as pl
from jax.experimental.pallas import tpu as pltpu
from jax.experimental.layout import Layout, with_layout_constraint
from jax.sharding import PartitionSpec as P


NZ, NX, NC, NL, NY = 4, 4, 2, 2, 4
EPS = 1e-05

Y_GROUPS = [[l * NY + y for y in range(NY)] for l in range(NL)]
PIECES = (0, 1, 3, 2)


def dp_send(value, dz=0, dx=0, dc=0):
    pairs = []
    for z in range(NZ):
        for x in range(NX):
            for c in range(NC):
                to = (((z + dz) % NZ) * NX + (x + dx) % NX) * NC + (c + dc) % NC
                pairs.append(((z * NX + x) * NC + c, to))
    return lax.ppermute(value, "dp", pairs)


def layer_swap(value):
    return lax.ppermute(value, "tensor", [(i, (i + NY) % (NL * NY)) for i in range(NL * NY)])


def exchange(value):
    return lax.all_to_all(value, "tensor", 0, 0, axis_index_groups=Y_GROUPS, tiled=True)


def rows_major(value):
    return with_layout_constraint(value, Layout(major_to_minor=tuple(range(value.ndim))))


def after(value, *earlier):
    return lax.optimization_barrier((value, earlier))[0]


def f32(v):
    return v.astype(jnp.float32)


def bf16(v):
    return v.astype(jnp.bfloat16)


def cat(*parts, axis=0):
    return jnp.concatenate(parts, axis=axis)


def half_select(first, second):
    width = first.shape[1] // 2
    lane = lax.broadcasted_iota(jnp.int32, first.shape, 1)
    low = jnp.where(lane < width, first, pltpu.roll(second, width, 1))
    high = jnp.where(lane < width, pltpu.roll(first, width, 1), second)
    return low, high


def block_at(dp, dx, dz, wide):
    z = lax.rem(dp // (NX * NC) + dz, NZ)
    x = lax.rem(lax.rem(dp // NC, NX) + dx, NX)
    return pl.ds(pl.multiple_of((z * NX + x) * wide, wide), wide)


def unit_rows(quant_ref, resid_ref, scale_ref):
    summed = f32(resid_ref[...]) + f32(quant_ref[...]) * scale_ref[...]
    inverse = lax.rsqrt(jnp.mean(summed * summed, axis=-1, keepdims=True) + EPS)
    return summed * inverse, inverse


def norm_kernel(dp_ref, quant_ref, resid_ref, scale_ref, gain_ref, mine_ref, other_ref, work):
    dp = dp_ref[0]
    first = lax.rem(dp, NC) == 0
    wide = quant_ref.shape[1] // (NZ * NX)
    unit, _ = unit_rows(quant_ref, resid_ref, scale_ref)
    work[...] = unit * gain_ref[...]
    for k in range(NZ * NX // 2):
        pair = (work[:, block_at(dp, j // NZ, j % NZ, wide)] for j in (2 * k, 2 * k + 1))
        low, high = half_select(*pair)
        at = slice(k * wide, (k + 1) * wide)
        mine_ref[:, at] = bf16(jnp.where(first, low, high))
        other_ref[:, at] = bf16(jnp.where(first, high, low))


def grad_kernel(dp_ref, quant_ref, resid_ref, scale_ref, gain_ref, kept_ref, layer_ref, core_ref, out_ref, work):
    dp = dp_ref[0]
    first = lax.rem(dp, NC) == 0
    wide = quant_ref.shape[1] // (NZ * NX)
    for k in range(NZ * NX // 2):
        at = slice(k * wide, (k + 1) * wide)
        own, came = kept_ref[:, at] + f32(layer_ref[:, at]), f32(core_ref[:, at])
        pair = half_select(jnp.where(first, own, came), jnp.where(first, came, own))
        for j, block in zip((2 * k, 2 * k + 1), pair, strict=True):
            work[:, block_at(dp, PIECES[j // NZ], j % NZ, wide)] = block
    unit, inverse = unit_rows(quant_ref, resid_ref, scale_ref)
    term = gain_ref[...] * work[...]
    out_ref[...] = bf16(inverse * (term - unit * jnp.mean(unit * term, axis=-1, keepdims=True)))


def row_calls(dp, quant_rows, residual, row_scale, norm_gain):
    rows, width = quant_rows.shape
    tile = 16
    whole = lambda n: pl.BlockSpec((tile, n), lambda i, _: (i, 0))
    specs = [whole(width), whole(width), whole(1), pl.BlockSpec((1, width), lambda i, _: (0, 0))]
    args = (quant_rows, residual, row_scale.reshape(rows, 1), norm_gain.reshape(1, width))

    def call(kernel, extra, widths):
        return pl.pallas_call(
            kernel,
            out_shape=[jax.ShapeDtypeStruct((rows, n), jnp.bfloat16) for n in widths],
            grid_spec=pltpu.PrefetchScalarGridSpec(
                num_scalar_prefetch=1,
                grid=(rows // tile,),
                in_specs=specs + [whole(e.shape[1]) for e in extra],
                out_specs=[whole(n) for n in widths],
                scratch_shapes=[pltpu.VMEM((tile, width), jnp.float32)],
            ),
            cost_estimate=pl.CostEstimate(
                flops=20 * rows * width, bytes_accessed=10 * rows * width, transcendentals=rows
            ),
        )(dp, *args, *extra)

    return call


def hidden_kernel(gate_ref, up_ref, grad_ref, out_ref):
    width = gate_ref.shape[1]
    gate, up, grad = f32(gate_ref[...]), f32(up_ref[...]), f32(grad_ref[...])
    sig = 0.5 * jnp.tanh(0.5 * gate) + 0.5
    scaled = grad * sig
    out_ref[:, :width] = bf16(scaled * up * (1.0 + gate * (1.0 - sig)))
    out_ref[:, width:] = bf16(scaled * gate)


def hidden_call(gate_pre, up_pre, hidden_grad):
    rows, width = gate_pre.shape
    tile = rows // (NL * NY)
    return pl.pallas_call(
        hidden_kernel,
        out_shape=jax.ShapeDtypeStruct((rows, 2 * width), jnp.bfloat16),
        grid=(NL * NY,),
        in_specs=[pl.BlockSpec((tile, width), lambda i: (lax.rem(i, NL) * NY + i // NL, 0))] * 3,
        out_specs=pl.BlockSpec((tile, 2 * width), lambda i: (i, 0)),
        cost_estimate=pl.CostEstimate(
            flops=20 * rows * width, bytes_accessed=10 * rows * width, transcendentals=rows * width
        ),
    )(gate_pre, up_pre, hidden_grad)


def dot_t(a, b):
    return lax.dot_general(a, b, (((1,), (1,)), ((), ())), preferred_element_type=jnp.float32)


def dot_rows(a, b):
    return lax.dot_general(a, b, (((0,), (0,)), ((), ())), preferred_element_type=jnp.float32)


def gather_weights(weight):
    rows = weight.shape[0]
    z1, z3, z2 = dp_send(weight, dz=-1), dp_send(weight, dz=1), dp_send(weight, dz=2)
    w0 = cat(weight, z1, z2, z3)
    w1, w3 = dp_send(w0, dx=-1), dp_send(w0, dx=1)
    w2 = cat(dp_send(w1[: 2 * rows], dx=-1), dp_send(w3[2 * rows :], dx=1))
    return cat(w0, w1, w3, w2)


def gather_tokens(block, layer, *earlier):
    rows, width = block.shape
    came = layer_swap(block)
    pair = cat(jnp.where(layer == 0, block, came), jnp.where(layer == 0, came, block))
    spread = after(jnp.broadcast_to(pair, (NY, *pair.shape)), *earlier)
    return exchange(spread).reshape(NY * NL * rows, width)


def reduce_tokens(part, layer, earlier):
    rows, width = part.shape
    by_y = rows_major(exchange(after(rows_major(part).reshape(NY, rows // NY, width), earlier)))
    size = rows // (NY * NL)

    def total(which):
        return f32(lax.dynamic_slice_in_dim(by_y, which * size, size, 1)).sum(0)

    return total(layer), layer_swap(bf16(total(1 - layer))), by_y


def reduce_weights(part, factor):
    block = part.shape[0] // NX
    mid = block // 2

    def at(dx, first=0, last=block):
        return part[dx * block + first : dx * block + last]

    up, down = dp_send(at(2, 0, mid), dx=1), dp_send(at(2, mid), dx=-1)
    ahead = cat(bf16(f32(at(1, 0, mid)) + f32(up)), at(1, mid))
    behind = cat(at(3, 0, mid), bf16(f32(at(3, mid)) + f32(down)))
    from_down, from_up = dp_send(ahead, dx=1), dp_send(behind, dx=-1)
    total = f32(at(0)) + f32(from_down) + f32(from_up)
    rows = block // NZ
    got = [dp_send(bf16(total[k * rows : (k + 1) * rows]), dz=k) for k in (1, 3, 2)]
    return (total[:rows] + sum(f32(g) for g in got)) * factor


def body(
    quant_rows,
    residual,
    row_scale,
    norm_gain,
    gate_pre,
    up_pre,
    hidden_grad,
    gate_weight,
    up_weight,
):
    dp = lax.axis_index("dp").reshape(1)
    layer = lax.div(lax.axis_index("tensor"), NY)
    model_width = quant_rows.shape[1]
    half = model_width // NC
    width = gate_pre.shape[1]
    factor = 1.0 / math.sqrt(gate_pre.shape[0] * lax.axis_size("dp"))
    row_call = row_calls(dp, quant_rows, residual, row_scale, norm_gain)

    mine, other = row_call(norm_kernel, (), (half, half))
    theirs = dp_send(other, dc=1)
    weights = gather_weights(cat(gate_weight, up_weight, axis=1))
    grads = hidden_call(after(gate_pre, other), up_pre, hidden_grad)
    their_grads = dp_send(grads, dc=1)
    first = gather_tokens(mine, layer)
    normed = first, gather_tokens(theirs, layer, first)

    def weight_part(at):
        first = bf16(dot_rows(normed[0], grads[:, at]))
        return reduce_weights(bf16(dot_rows(normed[1], their_grads[:, at]) + f32(first)), factor)

    kept, came, moved = reduce_tokens(bf16(dot_t(their_grads, weights)), layer, normed[1])
    across = dp_send(bf16(kept + f32(came)), dc=1)
    own = reduce_tokens(bf16(dot_t(grads, weights)), layer, moved)[:2]
    gate_out, up_out = weight_part(slice(width)), weight_part(slice(width, None))
    (resid_grad,) = row_call(grad_kernel, (*own, across), (model_width,))
    return resid_grad, gate_out, up_out


def solution(mesh):
    rows, block = P(("dp", "tensor"), None), P("dp", "tensor")

    return jax.shard_map(
        body,
        mesh=mesh,
        in_specs=(rows, rows, P(("dp", "tensor")), P(), block, block, block, block, block),
        out_specs=(rows, block, block),
        check_vma=False,
    )
```

profile of v0, /device:TPU:8, one launch (start us, length us, event | category | flops | bytes accessed | tf_op | source)
XLA Modules:
  0.0 194.1 jit_solution(8971249011515540406)
XLA Ops:
  3.8 6.3 %collective-permute-start = (bf16[64,1792]{1,0:T(8,128)(2,1)S(1)}, bf16[64,1792]{1,0:T(8,128)(2,1)S(1)}, u32[]{:S(2)}, u32[]{:S(2)}) collective-permute-start(bf16[64,1792]{1,0:T(8,128)(2,1)S(1)} %get-tuple-element.41), channel_id=1, source_target_pairs={{0,192},{8,200},{16,208},{24,216},{32,224},{40,232},{48,240},{56,2... | collective-permute-start | bytes 688136 | tf_op jit(solution)/shard_map/ppermute | solution.py:26
  15.3 6.3 %shard_map.112 = (bf16[128,1024]{1,0:T(8,128)(2,1)}, bf16[128,1024]{1,0:T(8,128)(2,1)}) custom-call(s32[1]{0:T(128)} %bitcast.dp_ref, s32[128,2048]{1,0:T(8,128)} %quant_ref.3, bf16[128,2048]{1,0:T(8,128)(2,1)} %resid_ref.3, f32[128,1]{1,0:T(8,128)} %copy.13.scale_ref, f32[1,2048]{1,0:T(1,128)} %bitcast.19), custom_call_target="tpu_custom_call" | custom-call | flops 5242880 | bytes 2621440 | tf_op jit(solution)/shard_map/pallas_call | solution.py:114
  21.6 7.7 %shard_map.113 = bf16[1024,1792]{1,0:T(8,128)(2,1)} custom-call(bf16[1024,896]{1,0:T(8,128)(2,1)} %gate_ref, bf16[1024,896]{1,0:T(8,128)(2,1)} %up_ref.1, bf16[1024,896]{1,0:T(8,128)(2,1)} %grad_ref.1), custom_call_target="tpu_custom_call" | custom-call | flops 18350080 | bytes 9175040 | tf_op jit(solution)/shard_map/pallas_call | solution.py:144
  40.8 4.9 %all-to-all-start = ((bf16[4,256,1024]{2,1,0:T(8,128)(2,1)}), bf16[4,256,1024]{2,1,0:T(8,128)(2,1)S(1)}, u32[]{:S(2)}, u32[]{:S(2)}) async-start(bf16[4,256,1024]{2,1,0:T(8,128)(2,1)} %broadcast_in_dim.7), calls=%async_computation | async-start | bytes 4194304 | tf_op jit(solution)/shard_map/all_to_all | solution.py:34
  45.8 8.7 %collective-permute-done.3 = bf16[256,1792]{1,0:T(8,128)(2,1)S(1)} collective-permute-done((bf16[256,1792]{1,0:T(8,128)(2,1)}, bf16[256,1792]{1,0:T(8,128)(2,1)S(1)}, u32[]{:S(2)}, u32[]{:S(2)}) %collective-permute-start.3) | collective-permute-done | bytes 917536 | tf_op jit(solution)/shard_map/ppermute | solution.py:26
  54.5 3.7 %collective-permute-start.5 = (bf16[128,1792]{1,0:T(8,128)(2,1)S(1)}, bf16[128,1792]{1,0:T(8,128)(2,1)S(1)}, u32[]{:S(2)}, u32[]{:S(2)}) collective-permute-start(bf16[128,1792]{1,0:T(8,128)(2,1)S(1)} %slice.118), channel_id=1, source_target_pairs={{0,48},{8,56},{16,0},{24,8},{32,16},{40,24},{48,32},{56,40},{64,11... | collective-permute-start | bytes 1376264 | tf_op jit(solution)/shard_map/ppermute | solution.py:26
  60.8 6.3 %collective-permute-done.5 = bf16[128,1792]{1,0:T(8,128)(2,1)S(1)} collective-permute-done((bf16[128,1792]{1,0:T(8,128)(2,1)S(1)}, bf16[128,1792]{1,0:T(8,128)(2,1)S(1)}, u32[]{:S(2)}, u32[]{:S(2)}) %collective-permute-start.5) | collective-permute-done | bytes 458784 | tf_op jit(solution)/shard_map/ppermute | solution.py:26
  67.1 4.5 %collective-permute-done.6 = bf16[128,1792]{1,0:T(8,128)(2,1)S(1)} collective-permute-done((bf16[128,1792]{1,0:T(8,128)(2,1)S(1)}, bf16[128,1792]{1,0:T(8,128)(2,1)S(1)}, u32[]{:S(2)}, u32[]{:S(2)}) %collective-permute-start.6) | collective-permute-done | bytes 458784 | tf_op jit(solution)/shard_map/ppermute | solution.py:26
  73.6 5.2 %convolution_convert_fusion.1 = bf16[1024,1024]{1,0:T(8,128)(2,1)} fusion(bf16[1024,1792]{1,0:T(8,128)(2,1)S(1)} %copy-done, bf16[1024,1792]{1,0:T(8,128)(2,1)S(1)} %constant_dynamic-update-slice_fusion.2), kind=kOutput, calls=%fused_computation.5 | convolution fusion | flops 3759144960 | bytes 9437184 | tf_op jit(solution)/shard_map/dot_general | solution.py:157
  80.4 4.9 %all-to-all-start.1 = ((bf16[4,256,1024]{2,1,0:T(8,128)(2,1)}), bf16[4,256,1024]{2,1,0:T(8,128)(2,1)}, u32[]{:S(2)}, u32[]{:S(2)}) async-start(bf16[4,256,1024]{2,1,0:T(8,128)(2,1)} %broadcast_in_dim.6), calls=%async_computation.1 | async-start | bytes 4194304 | tf_op jit(solution)/shard_map/all_to_all | solution.py:34
  85.3 5.3 %fusion.4 = bf16[1024,896]{1,0:T(8,128)(2,1)} fusion(bf16[1024,1024]{1,0:T(8,128)(2,1)S(1)} %bitcast.17, bf16[1024,1792]{1,0:T(8,128)(2,1)} %shard_map.113), kind=kOutput, calls=%fused_computation.10 | convolution fusion | flops 1879048192 | bytes 5767168 | tf_op jit(solution)/shard_map/dot_general | solution.py:161
  90.6 3.7 %fusion = bf16[1024,896]{1,0:T(8,128)(2,1)} fusion(bf16[1024,1024]{1,0:T(8,128)(2,1)S(1)} %bitcast.18, bf16[1024,1792]{1,0:T(8,128)(2,1)S(1)} %copy-done.1), kind=kOutput, calls=%fused_computation.6 | convolution fusion | flops 1879048192 | bytes 5767168 | tf_op jit(solution)/shard_map/dot_general | solution.py:161
  94.3 7.3 %convolution_convert_fusion = bf16[1024,1024]{1,0:T(8,128)(2,1)} fusion(bf16[1024,1792]{1,0:T(8,128)(2,1)} %collective-permute-done.7, bf16[1024,1792]{1,0:T(8,128)(2,1)S(1)} %copy-done.9), kind=kOutput, calls=%fused_computation.4 | convolution fusion | flops 3759144960 | bytes 9437184 | tf_op jit(solution)/shard_map/dot_general | solution.py:157
  101.6 7.2 %all-to-all-done.1 = bf16[4,256,1024]{2,1,0:T(8,128)(2,1)} async-done(((bf16[4,256,1024]{2,1,0:T(8,128)(2,1)}), bf16[4,256,1024]{2,1,0:T(8,128)(2,1)}, u32[]{:S(2)}, u32[]{:S(2)}) %all-to-all-start.1) | async-done | bytes 2097184 | tf_op jit(solution)/shard_map/all_to_all | solution.py:34
  108.8 4.9 %all-to-all-start.2 = ((bf16[4,256,1024]{2,1,0:T(8,128)(2,1)}), bf16[4,256,1024]{2,1,0:T(8,128)(2,1)S(1)}, u32[]{:S(2)}, u32[]{:S(2)}) async-start(bf16[4,256,1024]{2,1,0:T(8,128)(2,1)} %bitcast.16), calls=%async_computation.2 | async-start | bytes 4194304 | tf_op jit(solution)/shard_map/all_to_all | solution.py:34
  113.7 5.2 %add_convert_fusion.1 = bf16[1024,896]{1,0:T(8,128)(2,1)S(1)} fusion(bf16[1024,896]{1,0:T(8,128)(2,1)} %fusion.4, bf16[1024,1024]{1,0:T(8,128)(2,1)} %bitcast.6, bf16[1024,1792]{1,0:T(8,128)(2,1)} %collective-permute-done.7), kind=kOutput, calls=%fused_computation.1 | convolution fusion | flops 1881800704 | bytes 7602176 | tf_op jit(solution)/shard_map/dot_general | solution.py:161
  122.3 4.6 %add_convert_fusion = bf16[1024,896]{1,0:T(8,128)(2,1)S(1)} fusion(bf16[1024,896]{1,0:T(8,128)(2,1)S(1)} %copy-done.10, bf16[1024,1024]{1,0:T(8,128)(2,1)} %bitcast.6, bf16[1024,1792]{1,0:T(8,128)(2,1)} %collective-permute-done.7), kind=kOutput, calls=%fused_computation | convolution fusion | flops 1881800704 | bytes 7602176 | tf_op jit(solution)/shard_map/dot_general | solution.py:161
  140.6 4.8 %all-to-all-start.3 = ((bf16[4,256,1024]{2,1,0:T(8,128)(2,1)}), bf16[4,256,1024]{2,1,0:T(8,128)(2,1)}, u32[]{:S(2)}, u32[]{:S(2)}) async-start(bf16[4,256,1024]{2,1,0:T(8,128)(2,1)} %bitcast.15), calls=%async_computation.3 | async-start | bytes 4194304 | tf_op jit(solution)/shard_map/all_to_all | solution.py:34
  148.5 6.2 %collective-permute-start.19 = (bf16[64,896]{1,0:T(8,128)(2,1)S(1)}, bf16[64,896]{1,0:T(8,128)(2,1)S(1)}, u32[]{:S(2)}, u32[]{:S(2)}) collective-permute-start(bf16[64,896]{1,0:T(8,128)(2,1)S(1)} %get-tuple-element.40), channel_id=1, source_target_pairs={{0,192},{8,200},{16,208},{24,216},{32,224},{40,232},{48,240},{56,2... | collective-permute-start | bytes 344072 | tf_op jit(solution)/shard_map/ppermute | solution.py:26
  159.5 3.5 %collective-permute-start.26 = (bf16[64,896]{1,0:T(8,128)(2,1)}, bf16[64,896]{1,0:T(8,128)(2,1)S(1)}, u32[]{:S(2)}, u32[]{:S(2)}) collective-permute-start(bf16[64,896]{1,0:T(8,128)(2,1)} %get-tuple-element.37), channel_id=1, source_target_pairs={{0,192},{8,200},{16,208},{24,216},{32,224},{40,232},{48,240},{56,2... | collective-permute-start | bytes 344072 | tf_op jit(solution)/shard_map/ppermute | solution.py:26
  163.7 4.1 %collective-permute-start.12 = (bf16[128,1024]{1,0:T(8,128)(2,1)S(1)}, bf16[128,1024]{1,0:T(8,128)(2,1)S(1)}, u32[]{:S(2)}, u32[]{:S(2)}) collective-permute-start(bf16[128,1024]{1,0:T(8,128)(2,1)S(1)} %dynamic-slice_reduce_fusion), channel_id=1, source_target_pairs={{0,4},{1,5},{2,6},{3,7},{4,0},{5,1},{6,2},{7,3},{8,12},{9,13},{10,... | collective-permute-start | bytes 786440 | tf_op jit(solution)/shard_map/ppermute | solution.py:30
  168.8 7.8 %collective-permute-done.12 = bf16[128,1024]{1,0:T(8,128)(2,1)S(1)} collective-permute-done((bf16[128,1024]{1,0:T(8,128)(2,1)S(1)}, bf16[128,1024]{1,0:T(8,128)(2,1)S(1)}, u32[]{:S(2)}, u32[]{:S(2)}) %collective-permute-start.12) | collective-permute-done | bytes 262176 | tf_op jit(solution)/shard_map/ppermute | solution.py:30
  182.0 4.9 %collective-permute-done.11.layer_ref = bf16[128,1024]{1,0:T(8,128)(2,1)S(1)} collective-permute-done((bf16[128,1024]{1,0:T(8,128)(2,1)S(1)}, bf16[128,1024]{1,0:T(8,128)(2,1)S(1)}, u32[]{:S(2)}, u32[]{:S(2)}) %collective-permute-start.11) | collective-permute-done | bytes 262176 | tf_op jit(solution)/shard_map/ppermute | solution.py:30
  187.6 6.5 %shard_map.114 = bf16[128,2048]{1,0:T(8,128)(2,1)} custom-call(s32[1]{0:T(128)} %bitcast.dp_ref, s32[128,2048]{1,0:T(8,128)} %quant_ref.3, bf16[128,2048]{1,0:T(8,128)(2,1)} %resid_ref.3, f32[128,1]{1,0:T(8,128)} %copy.13.scale_ref, f32[1,2048]{1,0:T(1,128)} %bitcast.20, f32[128,1024]{1,0:T(8,128)} %convert_reduce_fusion.1.kept_ref, ...), custom_call_target="tpu_custom_call" | custom-call | flops 5242880 | bytes 2621440 | tf_op jit(solution)/shard_map/pallas_call | solution.py:114
  (109 shorter events, 58.7 us)
Async XLA Ops:
  3.8 25.9 %collective-permute-start = (bf16[64,1792]{1,0:T(8,128)(2,1)S(1)}, bf16[64,1792]{1,0:T(8,128)(2,1)S(1)}, u32[]{:S(2)}, u32[]{:S(2)}) collective-permute-start(bf16[64,1792]{1,0:T(8,128)(2,1)S(1)} %get-tuple-element.41), channel_id=1, source_target_pairs={{0,192},{8,200},{16,208},{24,216},{32,224},{40,232},{48,240},{56,2... | collective-permute-start | bytes 688136 | tf_op jit(solution)/shard_map/ppermute | solution.py:26
  10.1 20.7 %collective-permute-start.1 = (bf16[64,1792]{1,0:T(8,128)(2,1)S(1)}, bf16[64,1792]{1,0:T(8,128)(2,1)S(1)}, u32[]{:S(2)}, u32[]{:S(2)}) collective-permute-start(bf16[64,1792]{1,0:T(8,128)(2,1)S(1)} %get-tuple-element.41), channel_id=1, source_target_pairs={{0,128},{8,136},{16,144},{24,152},{32,160},{40,168},{48,176},{56,1... | collective-permute-start | bytes 688136 | tf_op jit(solution)/shard_map/ppermute | solution.py:26
  11.0 19.8 %collective-permute-start.2 = (bf16[64,1792]{1,0:T(8,128)(2,1)S(1)}, bf16[64,1792]{1,0:T(8,128)(2,1)S(1)}, u32[]{:S(2)}, u32[]{:S(2)}) collective-permute-start(bf16[64,1792]{1,0:T(8,128)(2,1)S(1)} %get-tuple-element.41), channel_id=1, source_target_pairs={{0,64},{8,72},{16,80},{24,88},{32,96},{40,104},{48,112},{56,120},{... | collective-permute-start | bytes 688136 | tf_op jit(solution)/shard_map/ppermute | solution.py:26
  21.6 15.2 %collective-permute-start.8 = (bf16[128,1024]{1,0:T(8,128)(2,1)}, bf16[128,1024]{1,0:T(8,128)(2,1)S(1)}, u32[]{:S(2)}, u32[]{:S(2)}) collective-permute-start(bf16[128,1024]{1,0:T(8,128)(2,1)} %get-tuple-element.9), channel_id=1, source_target_pairs={{0,8},{8,0},{16,24},{24,16},{32,40},{40,32},{48,56},{56,48},{64,72... | collective-permute-start | bytes 786440 | tf_op jit(solution)/shard_map/ppermute | solution.py:26
  29.3 65.0 %collective-permute-start.7 = (bf16[1024,1792]{1,0:T(8,128)(2,1)}, bf16[1024,1792]{1,0:T(8,128)(2,1)}, u32[]{:S(2)}, u32[]{:S(2)}) collective-permute-start(bf16[1024,1792]{1,0:T(8,128)(2,1)} %shard_map.113), channel_id=1, source_target_pairs={{0,8},{8,0},{16,24},{24,16},{32,40},{40,32},{48,56},{56,48},{64,72... | collective-permute-start | bytes 11010056 | tf_op jit(solution)/shard_map/ppermute | solution.py:26
  31.8 22.7 %collective-permute-start.3 = (bf16[256,1792]{1,0:T(8,128)(2,1)}, bf16[256,1792]{1,0:T(8,128)(2,1)S(1)}, u32[]{:S(2)}, u32[]{:S(2)}) collective-permute-start(bf16[256,1792]{1,0:T(8,128)(2,1)} %pad_maximum_fusion), channel_id=1, source_target_pairs={{0,48},{8,56},{16,0},{24,8},{32,16},{40,24},{48,32},{56,40},{64,11... | collective-permute-start | bytes 2752520 | tf_op jit(solution)/shard_map/ppermute | solution.py:26
  34.6 23.6 %collective-permute-start.4 = (bf16[256,1792]{1,0:T(8,128)(2,1)}, bf16[256,1792]{1,0:T(8,128)(2,1)}, u32[]{:S(2)}, u32[]{:S(2)}) collective-permute-start(bf16[256,1792]{1,0:T(8,128)(2,1)} %pad_maximum_fusion), channel_id=1, source_target_pairs={{0,16},{8,24},{16,32},{24,40},{32,48},{40,56},{48,0},{56,8},{64,80... | collective-permute-start | bytes 2752520 | tf_op jit(solution)/shard_map/ppermute | solution.py:26
  40.8 38.0 %all-to-all-start = ((bf16[4,256,1024]{2,1,0:T(8,128)(2,1)}), bf16[4,256,1024]{2,1,0:T(8,128)(2,1)S(1)}, u32[]{:S(2)}, u32[]{:S(2)}) async-start(bf16[4,256,1024]{2,1,0:T(8,128)(2,1)} %broadcast_in_dim.7), calls=%async_computation | async-start | bytes 4194304 | tf_op jit(solution)/shard_map/all_to_all | solution.py:34
  54.5 12.6 %collective-permute-start.5 = (bf16[128,1792]{1,0:T(8,128)(2,1)S(1)}, bf16[128,1792]{1,0:T(8,128)(2,1)S(1)}, u32[]{:S(2)}, u32[]{:S(2)}) collective-permute-start(bf16[128,1792]{1,0:T(8,128)(2,1)S(1)} %slice.118), channel_id=1, source_target_pairs={{0,48},{8,56},{16,0},{24,8},{32,16},{40,24},{48,32},{56,40},{64,11... | collective-permute-start | bytes 1376264 | tf_op jit(solution)/shard_map/ppermute | solution.py:26
  59.2 12.4 %collective-permute-start.6 = (bf16[128,1792]{1,0:T(8,128)(2,1)S(1)}, bf16[128,1792]{1,0:T(8,128)(2,1)S(1)}, u32[]{:S(2)}, u32[]{:S(2)}) collective-permute-start(bf16[128,1792]{1,0:T(8,128)(2,1)S(1)} %slice.119), channel_id=1, source_target_pairs={{0,16},{8,24},{16,32},{24,40},{32,48},{40,56},{48,0},{56,8},{64,80... | collective-permute-start | bytes 1376264 | tf_op jit(solution)/shard_map/ppermute | solution.py:26
  80.4 28.4 %all-to-all-start.1 = ((bf16[4,256,1024]{2,1,0:T(8,128)(2,1)}), bf16[4,256,1024]{2,1,0:T(8,128)(2,1)}, u32[]{:S(2)}, u32[]{:S(2)}) async-start(bf16[4,256,1024]{2,1,0:T(8,128)(2,1)} %broadcast_in_dim.6), calls=%async_computation.1 | async-start | bytes 4194304 | tf_op jit(solution)/shard_map/all_to_all | solution.py:34
  108.8 31.8 %all-to-all-start.2 = ((bf16[4,256,1024]{2,1,0:T(8,128)(2,1)}), bf16[4,256,1024]{2,1,0:T(8,128)(2,1)S(1)}, u32[]{:S(2)}, u32[]{:S(2)}) async-start(bf16[4,256,1024]{2,1,0:T(8,128)(2,1)} %bitcast.16), calls=%async_computation.2 | async-start | bytes 4194304 | tf_op jit(solution)/shard_map/all_to_all | solution.py:34
  130.7 15.5 %collective-permute-start.17 = (bf16[256,896]{1,0:T(8,128)(2,1)S(1)}, bf16[256,896]{1,0:T(8,128)(2,1)}, u32[]{:S(2)}, u32[]{:S(2)}) collective-permute-start(bf16[256,896]{1,0:T(8,128)(2,1)S(1)} %pad_maximum_fusion.4), channel_id=1, source_target_pairs={{0,48},{8,56},{16,0},{24,8},{32,16},{40,24},{48,32},{56,40},{64,11... | collective-permute-start | bytes 1376264 | tf_op jit(solution)/shard_map/ppermute | solution.py:26
  131.6 15.3 %collective-permute-start.15 = (bf16[256,896]{1,0:T(8,128)(2,1)}, bf16[256,896]{1,0:T(8,128)(2,1)}, u32[]{:S(2)}, u32[]{:S(2)}) collective-permute-start(bf16[256,896]{1,0:T(8,128)(2,1)} %pad_maximum_fusion.3), channel_id=1, source_target_pairs={{0,16},{8,24},{16,32},{24,40},{32,48},{40,56},{48,0},{56,8},{64,80... | collective-permute-start | bytes 1376264 | tf_op jit(solution)/shard_map/ppermute | solution.py:26
  137.1 17.6 %collective-permute-start.24 = (bf16[256,896]{1,0:T(8,128)(2,1)S(1)}, bf16[256,896]{1,0:T(8,128)(2,1)}, u32[]{:S(2)}, u32[]{:S(2)}) collective-permute-start(bf16[256,896]{1,0:T(8,128)(2,1)S(1)} %pad_maximum_fusion.6), channel_id=1, source_target_pairs={{0,48},{8,56},{16,0},{24,8},{32,16},{40,24},{48,32},{56,40},{64,11... | collective-permute-start | bytes 1376264 | tf_op jit(solution)/shard_map/ppermute | solution.py:26
  140.5 14.3 %collective-permute-start.22 = (bf16[256,896]{1,0:T(8,128)(2,1)S(1)}, bf16[256,896]{1,0:T(8,128)(2,1)}, u32[]{:S(2)}, u32[]{:S(2)}) collective-permute-start(bf16[256,896]{1,0:T(8,128)(2,1)S(1)} %pad_maximum_fusion.5), channel_id=1, source_target_pairs={{0,16},{8,24},{16,32},{24,40},{32,48},{40,56},{48,0},{56,8},{64,80... | collective-permute-start | bytes 1376264 | tf_op jit(solution)/shard_map/ppermute | solution.py:26
  140.6 36.1 %all-to-all-start.3 = ((bf16[4,256,1024]{2,1,0:T(8,128)(2,1)}), bf16[4,256,1024]{2,1,0:T(8,128)(2,1)}, u32[]{:S(2)}, u32[]{:S(2)}) async-start(bf16[4,256,1024]{2,1,0:T(8,128)(2,1)} %bitcast.15), calls=%async_computation.3 | async-start | bytes 4194304 | tf_op jit(solution)/shard_map/all_to_all | solution.py:34
  148.4 14.8 %collective-permute-start.20 = (bf16[64,896]{1,0:T(8,128)(2,1)S(1)}, bf16[64,896]{1,0:T(8,128)(2,1)S(1)}, u32[]{:S(2)}, u32[]{:S(2)}) collective-permute-start(bf16[64,896]{1,0:T(8,128)(2,1)S(1)} %get-tuple-element.39), channel_id=1, source_target_pairs={{0,128},{8,136},{16,144},{24,152},{32,160},{40,168},{48,176},{56,1... | collective-permute-start | bytes 344072 | tf_op jit(solution)/shard_map/ppermute | solution.py:26
  148.5 15.2 %collective-permute-start.19 = (bf16[64,896]{1,0:T(8,128)(2,1)S(1)}, bf16[64,896]{1,0:T(8,128)(2,1)S(1)}, u32[]{:S(2)}, u32[]{:S(2)}) collective-permute-start(bf16[64,896]{1,0:T(8,128)(2,1)S(1)} %get-tuple-element.40), channel_id=1, source_target_pairs={{0,192},{8,200},{16,208},{24,216},{32,224},{40,232},{48,240},{56,2... | collective-permute-start | bytes 344072 | tf_op jit(solution)/shard_map/ppermute | solution.py:26
  154.7 13.1 %collective-permute-start.18 = (bf16[64,896]{1,0:T(8,128)(2,1)S(1)}, bf16[64,896]{1,0:T(8,128)(2,1)S(1)}, u32[]{:S(2)}, u32[]{:S(2)}) collective-permute-start(bf16[64,896]{1,0:T(8,128)(2,1)S(1)} %get-tuple-element.38), channel_id=1, source_target_pairs={{0,64},{8,72},{16,80},{24,88},{32,96},{40,104},{48,112},{56,120},{... | collective-permute-start | bytes 344072 | tf_op jit(solution)/shard_map/ppermute | solution.py:26
  156.9 22.0 %collective-permute-start.27 = (bf16[64,896]{1,0:T(8,128)(2,1)}, bf16[64,896]{1,0:T(8,128)(2,1)S(1)}, u32[]{:S(2)}, u32[]{:S(2)}) collective-permute-start(bf16[64,896]{1,0:T(8,128)(2,1)} %get-tuple-element.36), channel_id=1, source_target_pairs={{0,128},{8,136},{16,144},{24,152},{32,160},{40,168},{48,176},{56,1... | collective-permute-start | bytes 344072 | tf_op jit(solution)/shard_map/ppermute | solution.py:26
  159.5 19.4 %collective-permute-start.26 = (bf16[64,896]{1,0:T(8,128)(2,1)}, bf16[64,896]{1,0:T(8,128)(2,1)S(1)}, u32[]{:S(2)}, u32[]{:S(2)}) collective-permute-start(bf16[64,896]{1,0:T(8,128)(2,1)} %get-tuple-element.37), channel_id=1, source_target_pairs={{0,192},{8,200},{16,208},{24,216},{32,224},{40,232},{48,240},{56,2... | collective-permute-start | bytes 344072 | tf_op jit(solution)/shard_map/ppermute | solution.py:26
  163.2 15.8 %collective-permute-start.25 = (bf16[64,896]{1,0:T(8,128)(2,1)S(1)}, bf16[64,896]{1,0:T(8,128)(2,1)S(1)}, u32[]{:S(2)}, u32[]{:S(2)}) collective-permute-start(bf16[64,896]{1,0:T(8,128)(2,1)S(1)} %get-tuple-element.35), channel_id=1, source_target_pairs={{0,64},{8,72},{16,80},{24,88},{32,96},{40,104},{48,112},{56,120},{... | collective-permute-start | bytes 344072 | tf_op jit(solution)/shard_map/ppermute | solution.py:26
  163.7 12.8 %collective-permute-start.12 = (bf16[128,1024]{1,0:T(8,128)(2,1)S(1)}, bf16[128,1024]{1,0:T(8,128)(2,1)S(1)}, u32[]{:S(2)}, u32[]{:S(2)}) collective-permute-start(bf16[128,1024]{1,0:T(8,128)(2,1)S(1)} %dynamic-slice_reduce_fusion), channel_id=1, source_target_pairs={{0,4},{1,5},{2,6},{3,7},{4,0},{5,1},{6,2},{7,3},{8,12},{9,13},{10,... | collective-permute-start | bytes 786440 | tf_op jit(solution)/shard_map/ppermute | solution.py:30
  (19 other events, 158.0 us)
where the time goes:
time: 196 us; the launch traced here: 194 us
  starting transfers between devices  70.2 us (36%)
  waiting for transfers between devices  44.3 us (23%)
  matrix products  31.3 us (16%)
  Pallas kernels  20.5 us (10%)
  local copies, waits for them, and re-layouts  16 us (8%)
  other arithmetic  10.9 us (6%)
    ppermute x24, starting transfers between devices, dp_send(): return lax.ppermute(value, 'dp', pairs)  42.4 us
    ppermute x24, waiting for transfers between devices, dp_send(): return lax.ppermute(value, 'dp', pairs)  24.4 us
    all_to_all x4, starting transfers between devices, exchange(): lax.all_to_all(value, 'tensor', 0, 0, axis_index_groups=Y_GROUPS, tiled=T...  19.5 us
    dot_general x4, matrix products, dot_rows(): lax.dot_general(a, b, (((0,), (0,)), ((), ())), preferred_element_type=jn...  18.7 us
    pallas_call x2, Pallas kernels, call(): pl.pallas_call(kernel, out_shape=[jax.ShapeDtypeStruct((rows, n), jnp.bfl...  12.8 us
    ppermute x4, waiting for transfers between devices, layer_swap(): lax.ppermute(value, 'tensor', [(i, (i + NY) % (NL * NY)) for i in range(N...  12.7 us
    dot_general x2, matrix products, dot_t(): lax.dot_general(a, b, (((1,), (1,)), ((), ())), preferred_element_type=jn...  12.6 us
    ppermute x4, starting transfers between devices, layer_swap(): lax.ppermute(value, 'tensor', [(i, (i + NY) % (NL * NY)) for i in range(N...  8.32 us
  transfers between devices with their start and end apart: 32, of which 9 were waited for; matrix products, arithmetic and copies ran while one was open for 27% of the time, Pallas kernels for 7%

commit v1 on v0

v1 whole, which is shorter than its diff:
```python
import math

import jax
import jax.numpy as jnp
from jax import lax
from jax.experimental import pallas as pl
from jax.experimental.pallas import tpu as pltpu
from jax.experimental.layout import Layout, with_layout_constraint
from jax.sharding import PartitionSpec as P


NZ, NX, NC, NL, NY = 4, 4, 2, 2, 4
EPS = 1e-05

PIECES = (0, 1, 3, 2)


def dp_send(value, dz=0, dx=0, dc=0):
    pairs = []
    for z in range(NZ):
        for x in range(NX):
            for c in range(NC):
                to = (((z + dz) % NZ) * NX + (x + dx) % NX) * NC + (c + dc) % NC
                pairs.append(((z * NX + x) * NC + c, to))
    return lax.ppermute(value, "dp", pairs)


def tensor_send(value, dl=0, dy=0):
    pairs = []
    for l in range(NL):
        for y in range(NY):
            pairs.append((l * NY + y, ((l + dl) % NL) * NY + (y + dy) % NY))
    return lax.ppermute(value, "tensor", pairs)


def rows_major(value):
    return with_layout_constraint(value, Layout(major_to_minor=tuple(range(value.ndim))))


def after(value, *earlier):
    return lax.optimization_barrier((value, earlier))[0]


def f32(v):
    return v.astype(jnp.float32)


def bf16(v):
    return v.astype(jnp.bfloat16)


def cat(*parts, axis=0):
    return jnp.concatenate(parts, axis=axis)


def half_select(first, second):
    width = first.shape[1] // 2
    lane = lax.broadcasted_iota(jnp.int32, first.shape, 1)
    low = jnp.where(lane < width, first, pltpu.roll(second, width, 1))
    high = jnp.where(lane < width, pltpu.roll(first, width, 1), second)
    return low, high


def block_at(dp, dx, dz, wide):
    z = lax.rem(dp // (NX * NC) + dz, NZ)
    x = lax.rem(lax.rem(dp // NC, NX) + dx, NX)
    return pl.ds(pl.multiple_of((z * NX + x) * wide, wide), wide)


CHUNK = 16


def unit_rows(at, quant_ref, resid_ref, scale_ref):
    scale = scale_ref[0]
    row = at + lax.broadcasted_iota(jnp.int32, (CHUNK, scale.shape[1]), 0)
    lane = lax.broadcasted_iota(jnp.int32, (CHUNK, scale.shape[1]), 1)
    column = jnp.sum(jnp.where(row == lane, scale, 0.0), axis=1, keepdims=True)
    rows = pl.ds(at, CHUNK)
    summed = f32(resid_ref[rows, :]) + f32(quant_ref[rows, :]) * column
    inverse = lax.rsqrt(jnp.mean(summed * summed, axis=-1, keepdims=True) + EPS)
    return summed * inverse, inverse


def chunks(ref, step):
    def run(i, carry):
        step(pl.multiple_of(i * CHUNK, CHUNK))
        return carry

    lax.fori_loop(0, ref.shape[0] // CHUNK, run, 0)


def norm_kernel(dp_ref, quant_ref, resid_ref, scale_ref, gain_ref, gate_ref, up_ref, mine_ref, other_ref, weight_ref, work):
    dp = dp_ref[0]
    first = lax.rem(dp, NC) == 0
    wide = quant_ref.shape[1] // (NZ * NX)
    weight_ref[:, : gate_ref.shape[1]] = gate_ref[...]
    weight_ref[:, gate_ref.shape[1] :] = up_ref[...]

    def step(at):
        unit, _ = unit_rows(at, quant_ref, resid_ref, scale_ref)
        work[...] = unit * gain_ref[...]
        for k in range(NZ * NX // 2):
            pair = (work[:, block_at(dp, j // NZ, j % NZ, wide)] for j in (2 * k, 2 * k + 1))
            low, high = half_select(*pair)
            to = pl.ds(at, CHUNK), slice(k * wide, (k + 1) * wide)
            mine_ref[to] = bf16(jnp.where(first, low, high))
            other_ref[to] = bf16(jnp.where(first, high, low))

    chunks(quant_ref, step)


def grad_kernel(dp_ref, quant_ref, resid_ref, scale_ref, gain_ref, kept_ref, layer_ref, core_ref, out_ref, work):
    dp = dp_ref[0]
    first = lax.rem(dp, NC) == 0
    wide = quant_ref.shape[1] // (NZ * NX)

    def step(at):
        rows = pl.ds(at, CHUNK)
        for k in range(NZ * NX // 2):
            part = rows, slice(k * wide, (k + 1) * wide)
            own, came = kept_ref[part] + f32(layer_ref[part]), f32(core_ref[part])
            pair = half_select(jnp.where(first, own, came), jnp.where(first, came, own))
            for j, block in zip((2 * k, 2 * k + 1), pair, strict=True):
                work[:, block_at(dp, PIECES[j // NZ], j % NZ, wide)] = block
        unit, inverse = unit_rows(at, quant_ref, resid_ref, scale_ref)
        term = gain_ref[...] * work[...]
        mean = jnp.mean(unit * term, axis=-1, keepdims=True)
        out_ref[rows, :] = bf16(inverse * (term - unit * mean))

    chunks(quant_ref, step)


def row_calls(dp, quant_rows, residual, row_scale, norm_gain):
    rows, width = quant_rows.shape
    steps = 2
    tile = rows // steps
    whole = lambda n, m: pl.BlockSpec((m // steps, n), lambda i, _: (i, 0))
    specs = [
        whole(width, rows),
        whole(width, rows),
        pl.BlockSpec((1, 1, tile), lambda i, _: (i, 0, 0)),
        pl.BlockSpec((1, width), lambda i, _: (0, 0)),
    ]
    args = (quant_rows, residual, row_scale.reshape(steps, 1, tile), norm_gain.reshape(1, width))

    def call(kernel, extra, outs):
        return pl.pallas_call(
            kernel,
            out_shape=[jax.ShapeDtypeStruct(o, jnp.bfloat16) for o in outs],
            grid_spec=pltpu.PrefetchScalarGridSpec(
                num_scalar_prefetch=1,
                grid=(steps,),
                in_specs=specs + [whole(e.shape[1], e.shape[0]) for e in extra],
                out_specs=[whole(n, m) for m, n in outs],
                scratch_shapes=[pltpu.VMEM((CHUNK, width), jnp.float32)],
            ),
            cost_estimate=pl.CostEstimate(
                flops=20 * rows * width, bytes_accessed=10 * rows * width, transcendentals=rows
            ),
        )(dp, *args, *extra)

    return call


def hidden_kernel(tensor_ref, gate_ref, up_ref, grad_ref, out_ref):
    width = gate_ref.shape[1]
    gate, up, grad = f32(gate_ref[...]), f32(up_ref[...]), f32(grad_ref[...])
    sig = 0.5 * jnp.tanh(0.5 * gate) + 0.5
    scaled = grad * sig
    out_ref[:, :width] = bf16(scaled * up * (1.0 + gate * (1.0 - sig)))
    out_ref[:, width:] = bf16(scaled * gate)


def hidden_call(tensor, gate_pre, up_pre, hidden_grad):
    rows, width = gate_pre.shape
    tile = rows // (NL * NY)

    def source(i, tensor_ref):
        l = lax.rem(lax.div(tensor_ref[0], NY) + lax.rem(i, NL), NL)
        y = lax.rem(lax.rem(tensor_ref[0], NY) + lax.div(i, NL), NY)
        return (l * NY + y, 0)

    return pl.pallas_call(
        hidden_kernel,
        out_shape=jax.ShapeDtypeStruct((rows, 2 * width), jnp.bfloat16),
        grid_spec=pltpu.PrefetchScalarGridSpec(
            num_scalar_prefetch=1,
            grid=(NL * NY,),
            in_specs=[pl.BlockSpec((tile, width), source)] * 3,
            out_specs=pl.BlockSpec((tile, 2 * width), lambda i, _: (i, 0)),
        ),
        cost_estimate=pl.CostEstimate(
            flops=20 * rows * width, bytes_accessed=10 * rows * width, transcendentals=rows * width
        ),
    )(tensor, gate_pre, up_pre, hidden_grad)


def dot_t(a, b):
    return lax.dot_general(a, b, (((1,), (1,)), ((), ())), preferred_element_type=jnp.float32)


def dot_rows(a, b):
    return lax.dot_general(a, b, (((0,), (0,)), ((), ())), preferred_element_type=jnp.float32)


def weight_kernel(normed_ref, their_normed_ref, grad_ref, their_grad_ref, out_ref):
    out_ref[...] = bf16(
        dot_rows(normed_ref[...], grad_ref[...]) + dot_rows(their_normed_ref[...], their_grad_ref[...])
    )


def weight_call(normed, grads, column):
    tokens, rows = normed[0].shape
    width = grads[0].shape[1] // 2
    tile = rows // 4
    return pl.pallas_call(
        weight_kernel,
        out_shape=jax.ShapeDtypeStruct((rows, width), jnp.bfloat16),
        grid=(rows // tile,),
        in_specs=[pl.BlockSpec((tokens, tile), lambda i: (0, i))] * 2
        + [pl.BlockSpec((tokens, width), lambda i: (0, column))] * 2,
        out_specs=pl.BlockSpec((tile, width), lambda i: (i, 0)),
        cost_estimate=pl.CostEstimate(
            flops=4 * tokens * rows * width,
            bytes_accessed=2 * (2 * tokens + width) * rows + 8 * tokens * width,
            transcendentals=0,
        ),
    )(*normed, *grads)


def gather_weights(weight):
    rows = weight.shape[0]
    z1, z3, z2 = dp_send(weight, dz=-1), dp_send(weight, dz=1), dp_send(weight, dz=2)
    w0 = cat(weight, z1, z2, z3)
    w1, w3 = dp_send(w0, dx=-1), dp_send(w0, dx=1)
    w2 = cat(dp_send(w1[: 2 * rows], dx=-1), dp_send(w3[2 * rows :], dx=1))
    return cat(w0, w1, w3, w2)


def gather_tokens(mine, theirs):
    rows = mine.shape[0]
    came = tensor_send(cat(mine, theirs), dl=1)
    n0 = cat(mine, came[:rows], theirs, came[rows:])
    half = 2 * rows
    n1, n3 = tensor_send(n0, dy=-1), tensor_send(n0, dy=1)
    far = tensor_send(n1[:half], dy=-1), tensor_send(n3[half:], dy=1)
    return tuple(
        cat(n0[at], n1[at], middle, n3[at])
        for at, middle in zip((slice(half), slice(half, None)), far, strict=True)
    )


def reduce_tokens(theirs, own):
    rows = own.shape[0] // NY
    at = lambda part, dy: part[dy * rows : (dy + 1) * rows]
    t_far, t_back = tensor_send(at(theirs, 2), dy=1), tensor_send(at(theirs, 3), dy=-1)
    o_far, o_ahead = tensor_send(at(own, 2), dy=-1), tensor_send(at(own, 1), dy=1)
    t_ahead = tensor_send(bf16(f32(at(theirs, 1)) + f32(t_far)), dy=1)
    o_back = tensor_send(bf16(f32(at(own, 3)) + f32(o_far)), dy=-1)
    results = []
    for part, *got in ((theirs, t_back, t_ahead), (own, o_ahead, o_back)):
        total = lambda where: sum(f32(v[where]) for v in (at(part, 0), *got))
        came = tensor_send(bf16(total(slice(rows // NL, None))), dl=1)
        results.append((total(slice(rows // NL)), came))
    return results


def reduce_weights(part, factor):
    block = part.shape[0] // NX
    mid = block // 2

    def at(dx, first=0, last=block):
        return part[dx * block + first : dx * block + last]

    up, down = dp_send(at(2, 0, mid), dx=1), dp_send(at(2, mid), dx=-1)
    ahead = cat(bf16(f32(at(1, 0, mid)) + f32(up)), at(1, mid))
    behind = cat(at(3, 0, mid), bf16(f32(at(3, mid)) + f32(down)))
    from_down, from_up = dp_send(ahead, dx=1), dp_send(behind, dx=-1)
    total = f32(at(0)) + f32(from_down) + f32(from_up)
    rows = block // NZ
    got = [dp_send(bf16(total[k * rows : (k + 1) * rows]), dz=k) for k in (1, 3, 2)]
    return (total[:rows] + sum(f32(g) for g in got)) * factor


def body(
    quant_rows,
    residual,
    row_scale,
    norm_gain,
    gate_pre,
    up_pre,
    hidden_grad,
    gate_weight,
    up_weight,
):
    dp = lax.axis_index("dp").reshape(1)
    tensor = lax.axis_index("tensor").reshape(1)
    rows, model_width = quant_rows.shape
    width = gate_pre.shape[1]
    factor = 1.0 / math.sqrt(gate_pre.shape[0] * lax.axis_size("dp"))
    row_call = row_calls(dp, quant_rows, residual, row_scale, norm_gain)

    block = (rows, model_width // NC)
    mine, other, weight = row_call(
        norm_kernel, (gate_weight, up_weight), (block, block, (gate_weight.shape[0], 2 * width))
    )
    theirs = dp_send(other, dc=1)
    weights = gather_weights(weight)
    grads = hidden_call(tensor, after(gate_pre, other), up_pre, hidden_grad)
    their_grads = dp_send(grads, dc=1)
    normed = gather_tokens(mine, theirs)

    their_part = rows_major(bf16(dot_t(their_grads, weights)))
    own_part = rows_major(bf16(dot_t(grads, weights)))
    (kept, came), own = reduce_tokens(their_part, own_part)
    across = dp_send(bf16(kept + f32(came)), dc=1)
    outs = []
    for h in range(2):
        part = weight_call(normed, (grads, their_grads), h)
        outs.append(reduce_weights(part, factor))
    (resid_grad,) = row_call(grad_kernel, (*own, across), ((rows, model_width),))
    return resid_grad, *outs


def solution(mesh):
    rows, block = P(("dp", "tensor"), None), P("dp", "tensor")

    return jax.shard_map(
        body,
        mesh=mesh,
        in_specs=(rows, rows, P(("dp", "tensor")), P(), block, block, block, block, block),
        out_specs=(rows, block, block),
        check_vma=False,
    )
```

time: 196 us -> 219 us (1.12); the launches traced: 194 us -> 215 us
  waiting for transfers between devices: 44.3 us -> 90 us
  matrix products: 31.3 us -> 11.3 us
  Pallas kernels: 20.5 us -> 33.7 us
  starting transfers between devices: 70.2 us -> 62.6 us
  other arithmetic: 10.9 us -> 4.04 us
  local copies, waits for them, and re-layouts: 16 us -> 11.8 us
    ppermute x4 -> x13, waiting for transfers between devices: 12.7 us -> 44.1 us  [tensor_send(): return lax.ppermute(value, 'tensor', pairs)]
    ppermute x24, waiting for transfers between devices: 24.4 us -> 45.9 us  [dp_send(): return lax.ppermute(value, 'dp', pairs)]
    all_to_all x4 -> x0, starting transfers between devices: 19.5 us -> none  [exchange(): lax.all_to_all(value, 'tensor', 0, 0, axis_index_groups=Y_GROUPS, tiled=T...]
    dot_general x4 -> x0, matrix products: 18.7 us -> none  [dot_rows(): lax.dot_general(a, b, (((0,), (0,)), ((), ())), preferred_element_type=jn...]
    pallas_call x2 -> x4, Pallas kernels: 12.8 us -> 26.1 us  [the longest x2 17 us: weight_call(): pl.pallas_call(weight_kernel, out_shape=jax.ShapeDtypeStruct((rows, width...]
    all_to_all x4 -> x0, waiting for transfers between devices: 7.16 us -> none  [exchange(): lax.all_to_all(value, 'tensor', 0, 0, axis_index_groups=Y_GROUPS, tiled=T...]
    ppermute x4 -> x13, starting transfers between devices: 8.32 us -> 15.1 us  [tensor_send(): return lax.ppermute(value, 'tensor', pairs)]
    ppermute x24, starting transfers between devices: 42.4 us -> 47.6 us  [dp_send(): return lax.ppermute(value, 'dp', pairs)]
  transfers between devices with their start and end apart: 32 -> 37, of which waited for: 9 -> 13; matrix products, arithmetic and copies ran while one was open for 27% -> 11% of each run, Pallas kernels for 7% -> 11%
where the time goes in v1:
time: 219 us; the launch traced here: 215 us
  waiting for transfers between devices  90 us (41%)
  starting transfers between devices  62.6 us (29%)
  Pallas kernels  33.7 us (15%)
  local copies, waits for them, and re-layouts  11.8 us (5%)
  matrix products  11.3 us (5%)
  other arithmetic  4.04 us (2%)
    ppermute x24, starting transfers between devices, dp_send(): return lax.ppermute(value, 'dp', pairs)  47.6 us
    ppermute x24, waiting for transfers between devices, dp_send(): return lax.ppermute(value, 'dp', pairs)  45.9 us
    ppermute x13, waiting for transfers between devices, tensor_send(): return lax.ppermute(value, 'tensor', pairs)  44.1 us
    pallas_call x2, Pallas kernels, weight_call(): pl.pallas_call(weight_kernel, out_shape=jax.ShapeDtypeStruct((rows, width...  17 us
    ppermute x13, starting transfers between devices, tensor_send(): return lax.ppermute(value, 'tensor', pairs)  15.1 us
    dot_general x2, matrix products, dot_t(): lax.dot_general(a, b, (((1,), (1,)), ((), ())), preferred_element_type=jn...  11.3 us
    pallas_call x2, Pallas kernels, call(): pl.pallas_call(kernel, out_shape=[jax.ShapeDtypeStruct(o, jnp.bfloat16) f...  9.15 us
    pallas_call x1, Pallas kernels, hidden_call(): pl.pallas_call(hidden_kernel, out_shape=jax.ShapeDtypeStruct((rows, 2 * w...  7.64 us
  transfers between devices with their start and end apart: 37, of which 13 were waited for; matrix products, arithmetic and copies ran while one was open for 11% of the time, Pallas kernels for 11%

profile of v1, /device:TPU:8, one launch (start us, length us, event | category | flops | bytes accessed | tf_op | source)
XLA Modules:
  0.0 214.7 jit_solution(9609412768066588177)
XLA Ops:
  1.9 4.4 %shard_map.112 = (bf16[128,1024]{1,0:T(8,128)(2,1)}, bf16[128,1024]{1,0:T(8,128)(2,1)}, bf16[64,1792]{1,0:T(8,128)(2,1)}) custom-call(s32[1]{0:T(128)} %bitcast.dp_ref, s32[128,2048]{1,0:T(8,128)} %quant_ref.3, bf16[128,2048]{1,0:T(8,128)(2,1)} %resid_ref.3, f32[2,1,64]{2,1,0:T(1,128)} %bitcast.11, f32[1,2048]{1,0:T(1,128)} %bitcast.9, ...), custom_call_target="tpu_custom_call" | custom-call | flops 5242880 | bytes 2621440 | tf_op jit(solution)/shard_map/pallas_call | solution.py:147
  6.3 6.4 %collective-permute-start = (bf16[64,1792]{1,0:T(8,128)(2,1)}, bf16[64,1792]{1,0:T(8,128)(2,1)S(1)}, u32[]{:S(2)}, u32[]{:S(2)}) collective-permute-start(bf16[64,1792]{1,0:T(8,128)(2,1)} %get-tuple-element.9), channel_id=1, source_target_pairs={{0,192},{8,200},{16,208},{24,216},{32,224},{40,232},{48,240},{56,2... | collective-permute-start | bytes 688136 | tf_op jit(solution)/shard_map/ppermute | solution.py:25
  18.3 14.3 %collective-permute-done = bf16[64,1792]{1,0:T(8,128)(2,1)S(1)} collective-permute-done((bf16[64,1792]{1,0:T(8,128)(2,1)}, bf16[64,1792]{1,0:T(8,128)(2,1)S(1)}, u32[]{:S(2)}, u32[]{:S(2)}) %collective-permute-start) | collective-permute-done | bytes 229408 | tf_op jit(solution)/shard_map/ppermute | solution.py:25
  40.2 7.6 %shard_map.113.grad_ref = bf16[1024,1792]{1,0:T(8,128)(2,1)} custom-call(s32[1]{0:T(128)} %bitcast.3.tensor_ref, bf16[1024,896]{1,0:T(8,128)(2,1)} %gate_ref.2, bf16[1024,896]{1,0:T(8,128)(2,1)} %up_ref.3, bf16[1024,896]{1,0:T(8,128)(2,1)} %grad_ref.1), custom_call_target="tpu_custom_call" | custom-call | flops 18350080 | bytes 9175040 | tf_op jit(solution)/shard_map/pallas_call | solution.py:183
  50.2 8.7 %collective-permute-done.3 = bf16[256,1792]{1,0:T(8,128)(2,1)S(1)} collective-permute-done((bf16[256,1792]{1,0:T(8,128)(2,1)}, bf16[256,1792]{1,0:T(8,128)(2,1)S(1)}, u32[]{:S(2)}, u32[]{:S(2)}) %collective-permute-start.3) | collective-permute-done | bytes 917536 | tf_op jit(solution)/shard_map/ppermute | solution.py:25
  58.9 3.7 %collective-permute-start.5 = (bf16[128,1792]{1,0:T(8,128)(2,1)S(1)}, bf16[128,1792]{1,0:T(8,128)(2,1)S(1)}, u32[]{:S(2)}, u32[]{:S(2)}) collective-permute-start(bf16[128,1792]{1,0:T(8,128)(2,1)S(1)} %slice.212), channel_id=1, source_target_pairs={{0,48},{8,56},{16,0},{24,8},{32,16},{40,24},{48,32},{56,40},{64,11... | collective-permute-start | bytes 1376264 | tf_op jit(solution)/shard_map/ppermute | solution.py:25
  62.9 7.4 %collective-permute-done.5 = bf16[128,1792]{1,0:T(8,128)(2,1)S(1)} collective-permute-done((bf16[128,1792]{1,0:T(8,128)(2,1)S(1)}, bf16[128,1792]{1,0:T(8,128)(2,1)S(1)}, u32[]{:S(2)}, u32[]{:S(2)}) %collective-permute-start.5) | collective-permute-done | bytes 458784 | tf_op jit(solution)/shard_map/ppermute | solution.py:25
  70.3 3.5 %collective-permute-done.6 = bf16[128,1792]{1,0:T(8,128)(2,1)S(1)} collective-permute-done((bf16[128,1792]{1,0:T(8,128)(2,1)S(1)}, bf16[128,1792]{1,0:T(8,128)(2,1)S(1)}, u32[]{:S(2)}, u32[]{:S(2)}) %collective-permute-start.6) | collective-permute-done | bytes 458784 | tf_op jit(solution)/shard_map/ppermute | solution.py:25
  73.9 4.2 %convolution_convert_fusion.1 = bf16[1024,1024]{1,0:T(8,128)(2,1)S(1)} fusion(bf16[1024,1792]{1,0:T(8,128)(2,1)S(1)} %copy-done, bf16[1024,1792]{1,0:T(8,128)(2,1)S(1)} %constant_dynamic-update-slice_fusion.4), kind=kOutput, calls=%fused_computation.1 | convolution fusion | flops 3759144960 | bytes 9437184 | tf_op jit(solution)/shard_map/dot_general | solution.py:199
  82.9 10.2 %collective-permute-done.8 = bf16[256,1024]{1,0:T(8,128)(2,1)S(1)} collective-permute-done((bf16[256,1024]{1,0:T(8,128)(2,1)S(1)}, bf16[256,1024]{1,0:T(8,128)(2,1)S(1)}, u32[]{:S(2)}, u32[]{:S(2)}) %collective-permute-start.8) | collective-permute-done | bytes 524320 | tf_op jit(solution)/shard_map/ppermute | solution.py:33
  94.3 10.0 %collective-permute-done.20 = bf16[256,1024]{1,0:T(8,128)(2,1)S(1)} collective-permute-done((bf16[256,1024]{1,0:T(8,128)(2,1)S(1)}, bf16[256,1024]{1,0:T(8,128)(2,1)S(1)}, u32[]{:S(2)}, u32[]{:S(2)}) %collective-permute-start.20) | collective-permute-done | bytes 524320 | tf_op jit(solution)/shard_map/ppermute | solution.py:33
  104.5 6.7 %collective-permute-done.9 = bf16[256,1024]{1,0:T(8,128)(2,1)S(1)} collective-permute-done((bf16[256,1024]{1,0:T(8,128)(2,1)S(1)}, bf16[256,1024]{1,0:T(8,128)(2,1)S(1)}, u32[]{:S(2)}, u32[]{:S(2)}) %collective-permute-start.9) | collective-permute-done | bytes 524320 | tf_op jit(solution)/shard_map/ppermute | solution.py:33
  115.4 8.5 %shard_map.116 = bf16[1024,896]{1,0:T(8,128)(2,1)} custom-call(bf16[1024,1024]{1,0:T(8,128)(2,1)} %copy-done.6, bf16[1024,1024]{1,0:T(8,128)(2,1)} %copy-done.7, bf16[1024,1792]{1,0:T(8,128)(2,1)} %shard_map.113.grad_ref, bf16[1024,1792]{1,0:T(8,128)(2,1)} %copy-done.10), custom_call_target="tpu_custom_call" | custom-call | flops 3758096384 | bytes 13369344 | tf_op jit(solution)/shard_map/pallas_call | solution.py:216
  128.5 8.5 %shard_map.115 = bf16[1024,896]{1,0:T(8,128)(2,1)} custom-call(bf16[1024,1024]{1,0:T(8,128)(2,1)} %copy-done.6, bf16[1024,1024]{1,0:T(8,128)(2,1)} %copy-done.7, bf16[1024,1792]{1,0:T(8,128)(2,1)} %shard_map.113.grad_ref, bf16[1024,1792]{1,0:T(8,128)(2,1)} %copy-done.10), custom_call_target="tpu_custom_call" | custom-call | flops 3758096384 | bytes 13369344 | tf_op jit(solution)/shard_map/pallas_call | solution.py:216
  141.7 7.1 %convolution_convert_fusion = bf16[1024,1024]{1,0:T(8,128)(2,1)S(1)} fusion(bf16[1024,1792]{1,0:T(8,128)(2,1)} %copy-done.10, bf16[1024,1792]{1,0:T(8,128)(2,1)} %copy-done.9), kind=kOutput, calls=%fused_computation | convolution fusion | flops 3759144960 | bytes 9437184 | tf_op jit(solution)/shard_map/dot_general | solution.py:199
  154.8 3.4 %collective-permute-done.13 = bf16[256,1024]{1,0:T(8,128)(2,1)S(1)} collective-permute-done((bf16[256,1024]{1,0:T(8,128)(2,1)S(1)}, bf16[256,1024]{1,0:T(8,128)(2,1)S(1)}, u32[]{:S(2)}, u32[]{:S(2)}) %collective-permute-start.13) | collective-permute-done | bytes 524320 | tf_op jit(solution)/shard_map/ppermute | solution.py:33
  158.4 7.1 %collective-permute-done.31 = bf16[256,896]{1,0:T(8,128)(2,1)S(1)} collective-permute-done((bf16[256,896]{1,0:T(8,128)(2,1)S(1)}, bf16[256,896]{1,0:T(8,128)(2,1)S(1)}, u32[]{:S(2)}, u32[]{:S(2)}) %collective-permute-start.31) | collective-permute-done | bytes 458784 | tf_op jit(solution)/shard_map/ppermute | solution.py:25
  167.6 4.7 %collective-permute-start.34 = (bf16[64,896]{1,0:T(8,128)(2,1)S(1)}, bf16[64,896]{1,0:T(8,128)(2,1)S(1)}, u32[]{:S(2)}, u32[]{:S(2)}) collective-permute-start(bf16[64,896]{1,0:T(8,128)(2,1)S(1)} %get-tuple-element.42), channel_id=1, source_target_pairs={{0,64},{8,72},{16,80},{24,88},{32,96},{40,104},{48,112},{56,120},{... | collective-permute-start | bytes 344072 | tf_op jit(solution)/shard_map/ppermute | solution.py:25
  172.3 3.3 %collective-permute-done.14 = bf16[256,1024]{1,0:T(8,128)(2,1)S(1)} collective-permute-done((bf16[256,1024]{1,0:T(8,128)(2,1)S(1)}, bf16[256,1024]{1,0:T(8,128)(2,1)S(1)}, u32[]{:S(2)}, u32[]{:S(2)}) %collective-permute-start.14) | collective-permute-done | bytes 524320 | tf_op jit(solution)/shard_map/ppermute | solution.py:33
  175.6 4.6 %collective-permute-start.35 = (bf16[64,896]{1,0:T(8,128)(2,1)S(1)}, bf16[64,896]{1,0:T(8,128)(2,1)S(1)}, u32[]{:S(2)}, u32[]{:S(2)}) collective-permute-start(bf16[64,896]{1,0:T(8,128)(2,1)S(1)} %get-tuple-element.44), channel_id=1, source_target_pairs={{0,192},{8,200},{16,208},{24,216},{32,224},{40,232},{48,240},{56,2... | collective-permute-start | bytes 344072 | tf_op jit(solution)/shard_map/ppermute | solution.py:25
  183.4 10.5 %collective-permute-done.15 = bf16[128,1024]{1,0:T(8,128)(2,1)S(1)} collective-permute-done((bf16[128,1024]{1,0:T(8,128)(2,1)S(1)}, bf16[128,1024]{1,0:T(8,128)(2,1)S(1)}, u32[]{:S(2)}, u32[]{:S(2)}) %collective-permute-start.15) | collective-permute-done | bytes 262176 | tf_op jit(solution)/shard_map/ppermute | solution.py:33
  194.0 4.1 %collective-permute-start.27 = (bf16[64,896]{1,0:T(8,128)(2,1)S(1)}, bf16[64,896]{1,0:T(8,128)(2,1)S(1)}, u32[]{:S(2)}, u32[]{:S(2)}) collective-permute-start(bf16[64,896]{1,0:T(8,128)(2,1)S(1)} %get-tuple-element.45), channel_id=1, source_target_pairs={{0,64},{8,72},{16,80},{24,88},{32,96},{40,104},{48,112},{56,120},{... | collective-permute-start | bytes 344072 | tf_op jit(solution)/shard_map/ppermute | solution.py:25
  198.4 4.5 %collective-permute-start.29 = (bf16[64,896]{1,0:T(8,128)(2,1)S(1)}, bf16[64,896]{1,0:T(8,128)(2,1)S(1)}, u32[]{:S(2)}, u32[]{:S(2)}) collective-permute-start(bf16[64,896]{1,0:T(8,128)(2,1)S(1)} %get-tuple-element.46), channel_id=1, source_target_pairs={{0,128},{8,136},{16,144},{24,152},{32,160},{40,168},{48,176},{56,1... | collective-permute-start | bytes 344072 | tf_op jit(solution)/shard_map/ppermute | solution.py:25
  210.0 4.8 %shard_map.114 = bf16[128,2048]{1,0:T(8,128)(2,1)} custom-call(s32[1]{0:T(128)} %bitcast.dp_ref, s32[128,2048]{1,0:T(8,128)} %quant_ref.3, bf16[128,2048]{1,0:T(8,128)(2,1)} %resid_ref.3, f32[2,1,64]{2,1,0:T(1,128)} %bitcast.12, f32[1,2048]{1,0:T(1,128)} %bitcast.10, f32[128,1024]{1,0:T(8,128)} %get-tuple-element.16.kept_ref, bf16[128,1024]{1,0:T(8,128)(2,1)} %copy-done.4, ...), custom_call_target="tpu_custom_call" | custom-call | flops 5242880 | bytes 2621440 | tf_op jit(solution)/shard_map/pallas_call | solution.py:147
  (121 shorter events, 55.3 us)
Async XLA Ops:
  6.3 26.3 %collective-permute-start = (bf16[64,1792]{1,0:T(8,128)(2,1)}, bf16[64,1792]{1,0:T(8,128)(2,1)S(1)}, u32[]{:S(2)}, u32[]{:S(2)}) collective-permute-start(bf16[64,1792]{1,0:T(8,128)(2,1)} %get-tuple-element.9), channel_id=1, source_target_pairs={{0,192},{8,200},{16,208},{24,216},{32,224},{40,232},{48,240},{56,2... | collective-permute-start | bytes 688136 | tf_op jit(solution)/shard_map/ppermute | solution.py:25
  12.7 20.8 %collective-permute-start.1 = (bf16[64,1792]{1,0:T(8,128)(2,1)}, bf16[64,1792]{1,0:T(8,128)(2,1)S(1)}, u32[]{:S(2)}, u32[]{:S(2)}) collective-permute-start(bf16[64,1792]{1,0:T(8,128)(2,1)} %get-tuple-element.9), channel_id=1, source_target_pairs={{0,128},{8,136},{16,144},{24,152},{32,160},{40,168},{48,176},{56,1... | collective-permute-start | bytes 688136 | tf_op jit(solution)/shard_map/ppermute | solution.py:25
  13.7 22.8 %collective-permute-start.2 = (bf16[64,1792]{1,0:T(8,128)(2,1)}, bf16[64,1792]{1,0:T(8,128)(2,1)S(1)}, u32[]{:S(2)}, u32[]{:S(2)}) collective-permute-start(bf16[64,1792]{1,0:T(8,128)(2,1)} %get-tuple-element.9), channel_id=1, source_target_pairs={{0,64},{8,72},{16,80},{24,88},{32,96},{40,104},{48,112},{56,120},{... | collective-permute-start | bytes 688136 | tf_op jit(solution)/shard_map/ppermute | solution.py:25
  16.5 17.8 %collective-permute-start.17 = (bf16[128,1024]{1,0:T(8,128)(2,1)}, bf16[128,1024]{1,0:T(8,128)(2,1)S(1)}, u32[]{:S(2)}, u32[]{:S(2)}) collective-permute-start(bf16[128,1024]{1,0:T(8,128)(2,1)} %get-tuple-element.7), channel_id=1, source_target_pairs={{0,8},{8,0},{16,24},{24,16},{32,40},{40,32},{48,56},{56,48},{64,72... | collective-permute-start | bytes 786440 | tf_op jit(solution)/shard_map/ppermute | solution.py:25
  37.4 21.5 %collective-permute-start.3 = (bf16[256,1792]{1,0:T(8,128)(2,1)}, bf16[256,1792]{1,0:T(8,128)(2,1)S(1)}, u32[]{:S(2)}, u32[]{:S(2)}) collective-permute-start(bf16[256,1792]{1,0:T(8,128)(2,1)} %get-tuple-element.48), channel_id=1, source_target_pairs={{0,48},{8,56},{16,0},{24,8},{32,16},{40,24},{48,32},{56,40},{64,11... | collective-permute-start | bytes 2752520 | tf_op jit(solution)/shard_map/ppermute | solution.py:25
  40.1 22.4 %collective-permute-start.4 = (bf16[256,1792]{1,0:T(8,128)(2,1)}, bf16[256,1792]{1,0:T(8,128)(2,1)S(1)}, u32[]{:S(2)}, u32[]{:S(2)}) collective-permute-start(bf16[256,1792]{1,0:T(8,128)(2,1)} %get-tuple-element.48), channel_id=1, source_target_pairs={{0,16},{8,24},{16,32},{24,40},{32,48},{40,56},{48,0},{56,8},{64,80... | collective-permute-start | bytes 2752520 | tf_op jit(solution)/shard_map/ppermute | solution.py:25
  47.8 65.8 %collective-permute-start.11 = (bf16[1024,1792]{1,0:T(8,128)(2,1)}, bf16[1024,1792]{1,0:T(8,128)(2,1)S(1)}, u32[]{:S(2)}, u32[]{:S(2)}) collective-permute-start(bf16[1024,1792]{1,0:T(8,128)(2,1)} %shard_map.113.grad_ref), channel_id=1, source_target_pairs={{0,8},{8,0},{16,24},{24,16},{32,40},{40,32},{48,56},{56,48},{64,72... | collective-permute-start | bytes 11010056 | tf_op jit(solution)/shard_map/ppermute | solution.py:25
  48.1 30.7 %collective-permute-start.19 = (bf16[512,1024]{1,0:T(8,128)(2,1)S(1)}, bf16[512,1024]{1,0:T(8,128)(2,1)S(1)}, u32[]{:S(2)}, u32[]{:S(2)}) collective-permute-start(bf16[512,1024]{1,0:T(8,128)(2,1)S(1)} %pad_maximum_fusion), channel_id=1, source_target_pairs={{0,3},{1,0},{2,1},{3,2},{4,7},{5,4},{6,5},{7,6},{8,11},{9,8},{10,9... | collective-permute-start | bytes 3145736 | tf_op jit(solution)/shard_map/ppermute | solution.py:33
  48.6 33.6 %collective-permute-start.21 = (bf16[512,1024]{1,0:T(8,128)(2,1)S(1)}, bf16[512,1024]{1,0:T(8,128)(2,1)S(1)}, u32[]{:S(2)}, u32[]{:S(2)}) collective-permute-start(bf16[512,1024]{1,0:T(8,128)(2,1)S(1)} %pad_maximum_fusion), channel_id=1, source_target_pairs={{0,1},{1,2},{2,3},{3,0},{4,5},{5,6},{6,7},{7,4},{8,9},{9,10},{10,1... | collective-permute-start | bytes 3145736 | tf_op jit(solution)/shard_map/ppermute | solution.py:33
  78.2 14.9 %collective-permute-start.8 = (bf16[256,1024]{1,0:T(8,128)(2,1)S(1)}, bf16[256,1024]{1,0:T(8,128)(2,1)S(1)}, u32[]{:S(2)}, u32[]{:S(2)}) collective-permute-start(bf16[256,1024]{1,0:T(8,128)(2,1)S(1)} %get-tuple-element.20), channel_id=1, source_target_pairs={{0,3},{1,0},{2,1},{3,2},{4,7},{5,4},{6,5},{7,6},{8,11},{9,8},{10,9... | collective-permute-start | bytes 1572872 | tf_op jit(solution)/shard_map/ppermute | solution.py:33
  78.9 25.4 %collective-permute-start.20 = (bf16[256,1024]{1,0:T(8,128)(2,1)S(1)}, bf16[256,1024]{1,0:T(8,128)(2,1)S(1)}, u32[]{:S(2)}, u32[]{:S(2)}) collective-permute-start(bf16[256,1024]{1,0:T(8,128)(2,1)S(1)} %get-tuple-element.37), channel_id=1, source_target_pairs={{0,3},{1,0},{2,1},{3,2},{4,7},{5,4},{6,5},{7,6},{8,11},{9,8},{10,9... | collective-permute-start | bytes 1572872 | tf_op jit(solution)/shard_map/ppermute | solution.py:33
  82.2 22.2 %collective-permute-start.22 = (bf16[256,1024]{1,0:T(8,128)(2,1)S(1)}, bf16[256,1024]{1,0:T(8,128)(2,1)S(1)}, u32[]{:S(2)}, u32[]{:S(2)}) collective-permute-start(bf16[256,1024]{1,0:T(8,128)(2,1)S(1)} %slice.237), channel_id=1, source_target_pairs={{0,1},{1,2},{2,3},{3,0},{4,5},{5,6},{6,7},{7,4},{8,9},{9,10},{10,1... | collective-permute-start | bytes 1572872 | tf_op jit(solution)/shard_map/ppermute | solution.py:33
  82.3 22.2 %collective-permute-start.7 = (bf16[256,1024]{1,0:T(8,128)(2,1)S(1)}, bf16[256,1024]{1,0:T(8,128)(2,1)S(1)}, u32[]{:S(2)}, u32[]{:S(2)}) collective-permute-start(bf16[256,1024]{1,0:T(8,128)(2,1)S(1)} %get-tuple-element.19), channel_id=1, source_target_pairs={{0,1},{1,2},{2,3},{3,0},{4,5},{5,6},{6,7},{7,4},{8,9},{9,10},{10,1... | collective-permute-start | bytes 1572872 | tf_op jit(solution)/shard_map/ppermute | solution.py:33
  93.3 18.0 %collective-permute-start.9 = (bf16[256,1024]{1,0:T(8,128)(2,1)S(1)}, bf16[256,1024]{1,0:T(8,128)(2,1)S(1)}, u32[]{:S(2)}, u32[]{:S(2)}) collective-permute-start(bf16[256,1024]{1,0:T(8,128)(2,1)S(1)} %add_convert_fusion.1), channel_id=1, source_target_pairs={{0,3},{1,0},{2,1},{3,2},{4,7},{5,4},{6,5},{7,6},{8,11},{9,8},{10,9... | collective-permute-start | bytes 1572872 | tf_op jit(solution)/shard_map/ppermute | solution.py:33
  112.3 96.9 %collective-permute-start.10 = (bf16[128,1024]{1,0:T(8,128)(2,1)S(1)}, bf16[128,1024]{1,0:T(8,128)(2,1)S(1)}, u32[]{:S(2)}, u32[]{:S(2)}) collective-permute-start(bf16[128,1024]{1,0:T(8,128)(2,1)S(1)} %get-tuple-element.15), channel_id=1, source_target_pairs={{0,4},{1,5},{2,6},{3,7},{4,0},{5,1},{6,2},{7,3},{8,12},{9,13},{10,... | collective-permute-start | bytes 786440 | tf_op jit(solution)/shard_map/ppermute | solution.py:33
  125.2 23.7 %collective-permute-start.30 = (bf16[128,896]{1,0:T(8,128)(2,1)S(1)}, bf16[128,896]{1,0:T(8,128)(2,1)S(1)}, u32[]{:S(2)}, u32[]{:S(2)}) collective-permute-start(bf16[128,896]{1,0:T(8,128)(2,1)S(1)} %get-tuple-element.23), channel_id=1, source_target_pairs={{0,16},{8,24},{16,32},{24,40},{32,48},{40,56},{48,0},{56,8},{64,80... | collective-permute-start | bytes 688136 | tf_op jit(solution)/shard_map/ppermute | solution.py:25
  125.3 25.3 %collective-permute-start.32 = (bf16[128,896]{1,0:T(8,128)(2,1)S(1)}, bf16[128,896]{1,0:T(8,128)(2,1)S(1)}, u32[]{:S(2)}, u32[]{:S(2)}) collective-permute-start(bf16[128,896]{1,0:T(8,128)(2,1)S(1)} %get-tuple-element.24), channel_id=1, source_target_pairs={{0,48},{8,56},{16,0},{24,8},{32,16},{40,24},{48,32},{56,40},{64,11... | collective-permute-start | bytes 688136 | tf_op jit(solution)/shard_map/ppermute | solution.py:25
  150.6 17.0 %collective-permute-start.12 = (bf16[256,1024]{1,0:T(8,128)(2,1)S(1)}, bf16[256,1024]{1,0:T(8,128)(2,1)S(1)}, u32[]{:S(2)}, u32[]{:S(2)}) collective-permute-start(bf16[256,1024]{1,0:T(8,128)(2,1)S(1)} %get-tuple-element.17), channel_id=1, source_target_pairs={{0,3},{1,0},{2,1},{3,2},{4,7},{5,4},{6,5},{7,6},{8,11},{9,8},{10,9... | collective-permute-start | bytes 1572872 | tf_op jit(solution)/shard_map/ppermute | solution.py:33
  151.3 14.2 %collective-permute-start.31 = (bf16[256,896]{1,0:T(8,128)(2,1)S(1)}, bf16[256,896]{1,0:T(8,128)(2,1)S(1)}, u32[]{:S(2)}, u32[]{:S(2)}) collective-permute-start(bf16[256,896]{1,0:T(8,128)(2,1)S(1)} %pad_maximum_fusion.4), channel_id=1, source_target_pairs={{0,16},{8,24},{16,32},{24,40},{32,48},{40,56},{48,0},{56,8},{64,80... | collective-permute-start | bytes 1376264 | tf_op jit(solution)/shard_map/ppermute | solution.py:25
  158.2 22.1 %collective-permute-start.24 = (bf16[256,896]{1,0:T(8,128)(2,1)S(1)}, bf16[256,896]{1,0:T(8,128)(2,1)S(1)}, u32[]{:S(2)}, u32[]{:S(2)}) collective-permute-start(bf16[256,896]{1,0:T(8,128)(2,1)S(1)} %pad_maximum_fusion.2), channel_id=1, source_target_pairs={{0,16},{8,24},{16,32},{24,40},{32,48},{40,56},{48,0},{56,8},{64,80... | collective-permute-start | bytes 1376264 | tf_op jit(solution)/shard_map/ppermute | solution.py:25
  165.5 17.7 %collective-permute-start.26 = (bf16[256,896]{1,0:T(8,128)(2,1)S(1)}, bf16[256,896]{1,0:T(8,128)(2,1)S(1)}, u32[]{:S(2)}, u32[]{:S(2)}) collective-permute-start(bf16[256,896]{1,0:T(8,128)(2,1)S(1)} %pad_maximum_fusion.3), channel_id=1, source_target_pairs={{0,48},{8,56},{16,0},{24,8},{32,16},{40,24},{48,32},{56,40},{64,11... | collective-permute-start | bytes 1376264 | tf_op jit(solution)/shard_map/ppermute | solution.py:25
  167.6 30.6 %collective-permute-start.34 = (bf16[64,896]{1,0:T(8,128)(2,1)S(1)}, bf16[64,896]{1,0:T(8,128)(2,1)S(1)}, u32[]{:S(2)}, u32[]{:S(2)}) collective-permute-start(bf16[64,896]{1,0:T(8,128)(2,1)S(1)} %get-tuple-element.42), channel_id=1, source_target_pairs={{0,64},{8,72},{16,80},{24,88},{32,96},{40,104},{48,112},{56,120},{... | collective-permute-start | bytes 344072 | tf_op jit(solution)/shard_map/ppermute | solution.py:25
  175.6 22.8 %collective-permute-start.35 = (bf16[64,896]{1,0:T(8,128)(2,1)S(1)}, bf16[64,896]{1,0:T(8,128)(2,1)S(1)}, u32[]{:S(2)}, u32[]{:S(2)}) collective-permute-start(bf16[64,896]{1,0:T(8,128)(2,1)S(1)} %get-tuple-element.44), channel_id=1, source_target_pairs={{0,192},{8,200},{16,208},{24,216},{32,224},{40,232},{48,240},{56,2... | collective-permute-start | bytes 344072 | tf_op jit(solution)/shard_map/ppermute | solution.py:25
  180.3 22.6 %collective-permute-start.36 = (bf16[64,896]{1,0:T(8,128)(2,1)S(1)}, bf16[64,896]{1,0:T(8,128)(2,1)S(1)}, u32[]{:S(2)}, u32[]{:S(2)}) collective-permute-start(bf16[64,896]{1,0:T(8,128)(2,1)S(1)} %get-tuple-element.43), channel_id=1, source_target_pairs={{0,128},{8,136},{16,144},{24,152},{32,160},{40,168},{48,176},{56,1... | collective-permute-start | bytes 344072 | tf_op jit(solution)/shard_map/ppermute | solution.py:25
  (24 other events, 227.3 us)
